TPU v7x, 128 devices: a whole 4x4x4 slice. The times are simulated.
128 devices in a mesh: gx: 8 (over x, core), gy: 16 (over z, y).
Axes of the slice: x: 4, y: 4, z: 4, core: 2. Of those that a mesh axis runs over, the one named last changes fastest.
Arguments:
- potential_heat: float32 [3, 384, 12288], P(None, 'gx', 'gy'), may hold values from -6 to 6
- easterly_speed: float32 [3, 384, 12288], P(None, 'gx', 'gy'), may hold values from -6 to 6
- poleward_speed: float32 [3, 384, 12288], P(None, 'gx', 'gy'), may hold values from -6 to 6
- sea_elevation: float32 [384, 12288], P('gx', 'gy'), may hold values from -6 to 6
- averaged_easterly_speed: float32 [384, 12288], P('gx', 'gy'), may hold values from -6 to 6
- averaged_poleward_speed: float32 [384, 12288], P('gx', 'gy'), may hold values from -6 to 6
- seafloor_distance: float32 [384, 12288], P('gx', 'gy'), may hold values from 0.5 to 2
- marine_indicator: int32 [384, 12288], P('gx', 'gy'), may hold values from 0 to 1, as said below
- hilbert_tile_sequence: int32 [1024], replicated, may hold values from -1 to 2047, as said below
Outputs:
- temp_next: float32 [3, 48, 49152], P(None, None, ('gx', 'gy'))
- zonal_next: float32 [3, 48, 49152], P(None, None, ('gx', 'gy'))
- merid_next: float32 [3, 48, 49152], P(None, None, ('gx', 'gy'))
- surface_next: float32 [48, 49152], P(None, ('gx', 'gy'))
- east_next: float32 [48, 49152], P(None, ('gx', 'gy'))
- north_next: float32 [48, 49152], P(None, ('gx', 'gy'))
Inputs may be any that keep to these rules, and one draw needn't show every extreme that they name: Slot s = (device index times 8) plus slot, with device index = gx index times the size of gy plus gy index, holds block hilbert_tile_sequence[s] = latitude row times 256 plus longitude column, or -1 if empty. Every block that hilbert_tile_sequence lists appears exactly once. A device's blocks all lie in the latitude row equal to its gx index, fill its first slots, and number at least one and at most 8; some device holds 8. `marine_indicator`: zero throughout every block that hilbert_tile_sequence does not list.
All inputs are finite; a program needn't handle non-finite values.
Results may differ from a plain program's by a relative error of at most 0.0003.
Values sent between devices are 32-bit elements; how exact they have to be, the bound alone decides.
No kernel may reach another device: no remote copies, remote signals or barrier semaphores. Data moves between devices by JAX's collectives and lax.ppermute only.
A program may use at most 128 MiB of HBM per device.

v0:
```python
import jax
import jax.numpy as jnp
from jax import lax
from jax.sharding import PartitionSpec as P

BAND = 16
SLOTS = 8
transport_factor = 0.4
spreading_factor = 0.1
time_coef = 0.3
viscous_coef = 0.1
quadratic_state_equation = 0.1
coriolis_amp = 0.5
surface_coef = 0.5
gravity_coef = 0.5


def with_halo(value, sides, width):
    for axis, dim in sides:
        size, length = (lax.axis_size(axis), value.shape[dim])
        up = [(i, (i + 1) % size) for i in range(size - 1)]
        down = [(j, i) for i, j in up]
        last = lax.slice_in_dim(value, length - width, length, axis=dim)
        initial = lax.slice_in_dim(value, 0, width, axis=dim)
        before = lax.ppermute(last, axis, up)
        after = lax.ppermute(initial, axis, down)
        value = jnp.concatenate([before, value, after], axis=dim)
    return value


def rolled(field, north, east):
    return jnp.roll(field, (-north, -east), axis=(-2, -1))


def easterly_biharmonic(field, displacement_helper):
    return (
        8.0 * (displacement_helper(field, 0, 1) - displacement_helper(field, 0, -1))
        - (displacement_helper(field, 0, 2) - displacement_helper(field, 0, -2))
    ) / 12.0


def poleward_biharmonic(field, displacement_helper):
    return (
        8.0 * (displacement_helper(field, 1, 0) - displacement_helper(field, -1, 0))
        - (displacement_helper(field, 2, 0) - displacement_helper(field, -2, 0))
    ) / 12.0


def east_centred(field, displacement_helper):
    return (displacement_helper(field, 0, 1) - displacement_helper(field, 0, -1)) * 0.5


def north_centred(field, displacement_helper):
    return (displacement_helper(field, 1, 0) - displacement_helper(field, -1, 0)) * 0.5


def second_difference(field, displacement_helper):
    return (
        displacement_helper(field, 0, 1)
        + displacement_helper(field, 0, -1)
        + (displacement_helper(field, 1, 0) + displacement_helper(field, -1, 0))
        - 4.0 * field
    )


def sheared_tendencies(marine_heat_values, westeast_watery, southnorth_watery, displacement_helper):
    transport_tendency = westeast_watery * easterly_biharmonic(
        marine_heat_values, displacement_helper
    ) + southnorth_watery * poleward_biharmonic(marine_heat_values, displacement_helper)
    spreading_tendency = second_difference(marine_heat_values, displacement_helper)
    density_anomaly = (
        marine_heat_values - quadratic_state_equation * marine_heat_values * marine_heat_values
    )
    pressure = jnp.cumsum(density_anomaly, axis=0)
    pressure = pressure - jnp.mean(pressure, axis=0)
    return (
        transport_tendency,
        spreading_tendency,
        east_centred(pressure, displacement_helper),
        north_centred(pressure, displacement_helper),
        second_difference(westeast_watery, displacement_helper),
        second_difference(southnorth_watery, displacement_helper),
    )


def barotropic_pass(
    height_now,
    flow_east,
    flow_north,
    depth_field,
    push_east,
    push_north,
    marine_points,
    displacement_helper,
):
    height_now = marine_points * (
        height_now
        - surface_coef
        * (
            east_centred(depth_field * flow_east, displacement_helper)
            + north_centred(depth_field * flow_north, displacement_helper)
        )
    )
    east_new = marine_points * (
        flow_east - gravity_coef * east_centred(height_now, displacement_helper) + push_east
    )
    north_new = marine_points * (
        flow_north - gravity_coef * north_centred(height_now, displacement_helper) + push_north
    )
    return (height_now, east_new, north_new)


def pick(rim_pool, pool_ids, wanted):
    matches = pool_ids[None, :] == wanted[:, None]
    located = jnp.any(matches, axis=1)
    position = jnp.sum(jnp.where(matches, jnp.arange(pool_ids.shape[0])[None, :], 0), axis=1)
    chosen = jnp.take(rim_pool, position, axis=0)
    return jnp.where(located[:, None, None], chosen, 0.0)


def curve_margin(fields, margin, slot_ids, table, row_index, move_rows, move_along):
    channels, tile_length, domain_span = fields.shape
    slot_count = domain_span // tile_length
    row_devices = lax.axis_size("gy")
    grid_rows = lax.axis_size("gx")
    blocks_east = BAND * row_devices
    grid = fields.reshape(channels, tile_length, slot_count, tile_length)

    def row_edge(edge):
        return edge.transpose(2, 1, 0, 3).reshape(slot_count, margin, channels * tile_length)

    def col_edge(edge):
        return edge.transpose(2, 3, 0, 1).reshape(slot_count, margin, channels * tile_length)

    south_edge = row_edge(grid[:, :margin])
    north_edge = row_edge(grid[:, tile_length - margin :])
    west_edge = col_edge(grid[..., :margin])
    east_edge = col_edge(grid[..., tile_length - margin :])
    across = move_rows(jnp.stack([south_edge, north_edge]))
    from_below, from_above, west_pool, east_pool = move_along(
        (across[0], across[3], west_edge, east_edge)
    )
    pool_size = row_devices * slot_count

    def row_ids(target_row):
        return lax.dynamic_slice(
            table, (jnp.clip(target_row, 0, grid_rows - 1) * pool_size,), (pool_size,)
        )

    own_ids = row_ids(row_index)
    below_ids = row_ids(row_index - 1)
    above_ids = row_ids(row_index + 1)
    in_use = slot_ids >= 0
    column = slot_ids % blocks_east
    has_south = in_use & (row_index > 0)
    has_north = in_use & (row_index < grid_rows - 1)
    has_west = column > 0
    has_east = column < blocks_east - 1
    want_south = jnp.where(has_south, slot_ids - blocks_east, -2)
    want_north = jnp.where(has_north, slot_ids + blocks_east, -2)
    want_west = jnp.where(in_use & has_west, slot_ids - 1, -2)
    want_east = jnp.where(in_use & has_east, slot_ids + 1, -2)
    want_south_west = jnp.where(has_south & has_west, slot_ids - blocks_east - 1, -2)
    want_south_east = jnp.where(has_south & has_east, slot_ids - blocks_east + 1, -2)
    want_north_west = jnp.where(has_north & has_west, slot_ids + blocks_east - 1, -2)
    want_north_east = jnp.where(has_north & has_east, slot_ids + blocks_east + 1, -2)

    def split_rim(rim):
        return rim.reshape(slot_count, margin, channels, tile_length)

    south_full = jnp.concatenate(
        [
            split_rim(pick(from_below, below_ids, want_south_west))[..., tile_length - margin :],
            split_rim(pick(from_below, below_ids, want_south)),
            split_rim(pick(from_below, below_ids, want_south_east))[..., :margin],
        ],
        axis=3,
    )
    north_full = jnp.concatenate(
        [
            split_rim(pick(from_above, above_ids, want_north_west))[..., tile_length - margin :],
            split_rim(pick(from_above, above_ids, want_north)),
            split_rim(pick(from_above, above_ids, want_north_east))[..., :margin],
        ],
        axis=3,
    )
    west_rim = pick(east_pool, own_ids, want_west)
    east_rim = pick(west_pool, own_ids, want_east)

    def col_back(rim):
        return rim.reshape(slot_count, margin, channels, tile_length).transpose(2, 3, 0, 1)

    middle = jnp.concatenate([col_back(west_rim), grid, col_back(east_rim)], axis=3)
    bordered_array = jnp.concatenate(
        [south_full.transpose(2, 1, 0, 3), middle, north_full.transpose(2, 1, 0, 3)], axis=1
    )
    return bordered_array.reshape(
        channels, tile_length + 2 * margin, slot_count * (tile_length + 2 * margin)
    )


def curve_inner(field, margin):
    leading = field.shape[:-2]
    padded_side = field.shape[-2]
    tile_length = padded_side - 2 * margin
    slot_count = field.shape[-1] // padded_side
    shaped = field.reshape(leading + (padded_side, slot_count, padded_side))
    shaped = shaped[..., margin : margin + tile_length, :, margin : margin + tile_length]
    return shaped.reshape(leading + (tile_length, slot_count * tile_length))


def relocate(stacked, slot_ids):
    channels, tile_length, domain_span = stacked.shape
    band_blocks = domain_span // tile_length
    row_devices = lax.axis_size("gy")
    blocks_east = band_blocks * row_devices
    slot_count = slot_ids.shape[0]
    columns_flat = stacked.reshape(channels * tile_length, domain_span)
    in_use = slot_ids >= 0
    column = jnp.where(in_use, slot_ids % blocks_east, -1)
    initial = jnp.zeros((channels * tile_length, slot_count, tile_length), jnp.float32)
    portion = lax.all_gather(columns_flat, "gy", axis=1, tiled=True)
    portion_blocks = portion.shape[1] // tile_length
    usable = in_use & (column >= 0) & (column < portion_blocks)
    taken = jnp.take(
        portion.reshape(channels * tile_length, portion_blocks, tile_length),
        jnp.clip(column, 0, portion_blocks - 1),
        axis=1,
    )
    gathered = jnp.where(usable[None, :, None], taken, initial)
    return gathered.reshape(channels, tile_length, slot_count * tile_length)


def advance(
    heat_tracer,
    zonal,
    merid,
    sea_elevation,
    east_flow,
    north_flow,
    depth_field,
    marine_points,
    coriolis,
    widen_sheared_halo,
    grow_twice,
    interior,
):
    layer_total = heat_tracer.shape[0]
    marine_heat_values = heat_tracer * marine_points
    westeast_watery = zonal * marine_points
    southnorth_watery = merid * marine_points
    bordered_array = widen_sheared_halo(
        jnp.concatenate([marine_heat_values, westeast_watery, southnorth_watery], axis=0), 2
    )
    terms = sheared_tendencies(
        bordered_array[:layer_total],
        bordered_array[layer_total : 2 * layer_total],
        bordered_array[2 * layer_total :],
        rolled,
    )
    (
        transport_tendency,
        spreading_tendency,
        easterly_gradient_force,
        poleward_gradient_force,
        easterly_friction,
        poleward_friction,
    ) = [interior(member, 2) for member in terms]
    updated_heat_tracer = marine_points * (
        marine_heat_values
        - transport_factor * transport_tendency
        + spreading_factor * spreading_tendency
    )
    zonal_new = marine_points * (
        westeast_watery
        + time_coef * (coriolis * southnorth_watery - easterly_gradient_force)
        + viscous_coef * easterly_friction
    )
    merid_new = marine_points * (
        southnorth_watery
        + time_coef * (-coriolis * westeast_watery - poleward_gradient_force)
        + viscous_coef * poleward_friction
    )
    push_east = jnp.mean(zonal_new - westeast_watery, axis=0)
    push_north = jnp.mean(merid_new - southnorth_watery, axis=0)
    height_now = sea_elevation * marine_points
    flow_east = east_flow * marine_points
    flow_north = north_flow * marine_points
    for sweep_index in range(2):
        bordered_array = grow_twice(
            jnp.stack(
                [
                    height_now,
                    flow_east,
                    flow_north,
                    depth_field,
                    push_east,
                    push_north,
                    marine_points,
                ]
            ),
            2,
        )
        result = barotropic_pass(
            bordered_array[0],
            bordered_array[1],
            bordered_array[2],
            bordered_array[3],
            bordered_array[4],
            bordered_array[5],
            bordered_array[6],
            rolled,
        )
        height_now, flow_east, flow_north = [interior(member, 2) for member in result]
    return (updated_heat_tracer, zonal_new, merid_new, height_now, flow_east, flow_north)


def shards(
    potential_heat,
    easterly_speed,
    poleward_speed,
    sea_elevation,
    averaged_easterly_speed,
    averaged_poleward_speed,
    seafloor_distance,
    marine_indicator,
    hilbert_tile_sequence,
):
    layer_total, tile_length, domain_span = potential_heat.shape
    grid_rows = lax.axis_size("gx")
    row_devices = lax.axis_size("gy")
    row_index = lax.axis_index("gx")
    device_flat = lax.axis_index(("gx", "gy"))
    slot_ids = lax.dynamic_slice(hilbert_tile_sequence, (device_flat * SLOTS,), (SLOTS,))
    marine_points = marine_indicator.astype(jnp.float32)
    grid_height = grid_rows * tile_length
    blocks_east = domain_span // tile_length * row_devices
    stacked = jnp.concatenate(
        [
            potential_heat,
            easterly_speed,
            poleward_speed,
            jnp.stack(
                [
                    sea_elevation,
                    averaged_easterly_speed,
                    averaged_poleward_speed,
                    seafloor_distance,
                    marine_points,
                ]
            ),
        ],
        axis=0,
    )
    moved = relocate(stacked, slot_ids)
    block_rows = slot_ids // blocks_east
    north_pos = (
        block_rows[None, :, None] * tile_length + jnp.arange(tile_length)[:, None, None]
    ).astype(jnp.float32)
    north_pos = jnp.broadcast_to(north_pos, (tile_length, SLOTS, tile_length)).reshape(
        tile_length, SLOTS * tile_length
    )
    coriolis = coriolis_amp * (2.0 * (north_pos + 0.5) / grid_height - 1.0)

    def widen_sheared_halo(fields, margin):

        def move_rows(edges):
            return with_halo(edges, (("gx", 0),), 1)

        def move_along(members):
            return lax.all_gather(members, "gy", axis=0, tiled=True)

        return curve_margin(
            fields, margin, slot_ids, hilbert_tile_sequence, row_index, move_rows, move_along
        )

    def grow_twice(fields, margin):

        def move_rows(edges):
            return with_halo(edges, (("gx", 0),), 1)

        def move_along(members):
            return lax.all_gather(members, "gy", axis=0, tiled=True)

        return curve_margin(
            fields, margin, slot_ids, hilbert_tile_sequence, row_index, move_rows, move_along
        )

    return advance(
        moved[:layer_total],
        moved[layer_total : 2 * layer_total],
        moved[2 * layer_total : 3 * layer_total],
        moved[3 * layer_total],
        moved[3 * layer_total + 1],
        moved[3 * layer_total + 2],
        moved[3 * layer_total + 3],
        moved[3 * layer_total + 4],
        coriolis,
        widen_sheared_halo,
        grow_twice,
        curve_inner,
    )


def solution(mesh):
    return jax.shard_map(
        shards,
        mesh=mesh,
        in_specs=(
            P(None, "gx", "gy"),
            P(None, "gx", "gy"),
            P(None, "gx", "gy"),
            P("gx", "gy"),
            P("gx", "gy"),
            P("gx", "gy"),
            P("gx", "gy"),
            P("gx", "gy"),
            P(),
        ),
        out_specs=(
            P(None, None, ("gx", "gy")),
            P(None, None, ("gx", "gy")),
            P(None, None, ("gx", "gy")),
            P(None, ("gx", "gy")),
            P(None, ("gx", "gy")),
            P(None, ("gx", "gy")),
        ),
        check_vma=False,
    )
```

profile of v0, /device:TPU:6, one launch (start us, length us, event | category | flops | bytes accessed | tf_op | source)
XLA Modules:
  0.0 768.4 jit_solution(7839690375137957721)
XLA Ops:
  23.1 209.6 %all-gather.8.cloned.1.call-done = f32[672,12288]{0,1:T(8,128)} async-done(((f32[672,768]{0,1:T(8,128)}), f32[672,12288]{0,1:T(8,128)}) %all-gather.8.cloned.1.call-update) | async-done | bytes 33030160 | tf_op jit(solution)/shard_map/all_gather | solution.py:222
  243.4 2.3 fusion.73
  245.7 2.1 copy.559
  247.8 26.0 %all_gather.42 = f32[128,2,432]{2,1,0:T(2,128)} all-gather(f32[8,2,432]{2,1,0:T(2,128)S(1)} %copy.559), channel_id=1, replica_groups=mesh['gx'=8,'gy'=16] {'gy'}, dimensions={0}, use_global_device_ids=true | all-gather | bytes 470016 | tf_op jit(solution)/shard_map/all_gather | solution.py:371
  273.9 2.1 copy.555
  275.9 23.7 %all_gather.41 = f32[128,2,432]{2,1,0:T(2,128)} all-gather(f32[8,2,432]{2,1,0:T(2,128)S(1)} %copy.555), channel_id=1, replica_groups=mesh['gx'=8,'gy'=16] {'gy'}, dimensions={0}, use_global_device_ids=true | all-gather | bytes 470016 | tf_op jit(solution)/shard_map/all_gather | solution.py:371
  315.8 23.5 %all-gather.1 = f32[1,128,2,432]{3,2,0,1:T(2,128)S(1)} all-gather(f32[1,8,2,432]{3,2,0,1:T(2,128)S(1)} %copy.563), channel_id=3, replica_groups=mesh['gx'=8,'gy'=16] {'gy'}, dimensions={1}, use_global_device_ids=true | all-gather | bytes 470016 | tf_op jit(solution)/shard_map/all_gather | solution.py:371
  342.5 23.9 %all-gather = f32[1,128,2,432]{3,2,0,1:T(2,128)} all-gather(f32[1,8,2,432]{3,2,0,1:T(2,128)S(1)} %copy.547), channel_id=2, replica_groups=mesh['gx'=8,'gy'=16] {'gy'}, dimensions={1}, use_global_device_ids=true | all-gather | bytes 470016 | tf_op jit(solution)/shard_map/all_gather | solution.py:371
  375.7 3.4 pad_maximum_fusion
  400.6 2.2 add.250
  403.5 2.1 concatenate.309
  408.1 3.0 fusion.1
  415.0 2.1 concatenate.305
  418.5 2.4 fusion.4
  422.9 2.5 fusion.18
  425.4 2.2 div.43
  434.3 2.1 concatenate.283
  436.4 2.1 concatenate.279
  442.3 2.2 concatenate.299
  446.6 2.1 concatenate.295
  450.6 2.1 add.244
  455.4 5.6 fusion.11
  472.2 2.5 subtract_reduce_fusion
  481.3 25.2 %all_gather.46 = f32[128,2,336]{2,1,0:T(2,128)} all-gather(f32[8,2,336]{2,1,0:T(2,128)S(1)} %reshape.804), channel_id=1, replica_groups=mesh['gx'=8,'gy'=16] {'gy'}, dimensions={0}, use_global_device_ids=true | all-gather | bytes 365568 | tf_op jit(solution)/shard_map/all_gather | solution.py:383
  508.5 23.7 %all_gather.45 = f32[128,2,336]{2,1,0:T(2,128)} all-gather(f32[8,2,336]{2,1,0:T(2,128)S(1)} %reshape.802), channel_id=1, replica_groups=mesh['gx'=8,'gy'=16] {'gy'}, dimensions={0}, use_global_device_ids=true | all-gather | bytes 365568 | tf_op jit(solution)/shard_map/all_gather | solution.py:383
  538.2 25.2 %all-gather.3 = f32[1,128,2,336]{3,2,0,1:T(2,128)} all-gather(f32[1,8,2,336]{3,2,0,1:T(2,128)S(1)} %copy.594), channel_id=5, replica_groups=mesh['gx'=8,'gy'=16] {'gy'}, dimensions={1}, use_global_device_ids=true | all-gather | bytes 365568 | tf_op jit(solution)/shard_map/all_gather | solution.py:383
  568.6 23.5 %all-gather.2 = f32[1,128,2,336]{3,2,0,1:T(2,128)} all-gather(f32[1,8,2,336]{3,2,0,1:T(2,128)S(1)} %copy.578), channel_id=4, replica_groups=mesh['gx'=8,'gy'=16] {'gy'}, dimensions={1}, use_global_device_ids=true | all-gather | bytes 365568 | tf_op jit(solution)/shard_map/all_gather | solution.py:383
  629.9 23.2 %all_gather.50 = f32[128,2,336]{2,1,0:T(2,128)S(1)} all-gather(f32[8,2,336]{2,1,0:T(2,128)S(1)} %reshape.819), channel_id=1, replica_groups=mesh['gx'=8,'gy'=16] {'gy'}, dimensions={0}, use_global_device_ids=true | all-gather | bytes 365568 | tf_op jit(solution)/shard_map/all_gather | solution.py:383
  654.1 21.8 %all_gather.49 = f32[128,2,336]{2,1,0:T(2,128)S(1)} all-gather(f32[8,2,336]{2,1,0:T(2,128)S(1)} %reshape.817), channel_id=1, replica_groups=mesh['gx'=8,'gy'=16] {'gy'}, dimensions={0}, use_global_device_ids=true | all-gather | bytes 365568 | tf_op jit(solution)/shard_map/all_gather | solution.py:383
  681.0 23.4 %all-gather.5 = f32[1,128,2,336]{3,2,0,1:T(2,128)S(1)} all-gather(f32[1,8,2,336]{3,2,0,1:T(2,128)S(1)} %copy.631), channel_id=7, replica_groups=mesh['gx'=8,'gy'=16] {'gy'}, dimensions={1}, use_global_device_ids=true | all-gather | bytes 365568 | tf_op jit(solution)/shard_map/all_gather | solution.py:383
  706.7 21.8 %all-gather.4 = f32[1,128,2,336]{3,2,0,1:T(2,128)S(1)} all-gather(f32[1,8,2,336]{3,2,0,1:T(2,128)S(1)} %copy.615), channel_id=6, replica_groups=mesh['gx'=8,'gy'=16] {'gy'}, dimensions={1}, use_global_device_ids=true | all-gather | bytes 365568 | tf_op jit(solution)/shard_map/all_gather | solution.py:383
  753.6 2.5 fusion.21
  (536 shorter events, 209.7 us)
Async XLA Ops:
  7.2 225.5 %all-gather.8.cloned.1.call-start = ((), (), s32[]{:S(2)}) async-start(), calls=%async_computation | async-start | bytes 40108032 | tf_op jit(solution)/shard_map/all_gather | solution.py:222
  12.8 221.8 %copy-start.31 = (f32[48,384]{1,0:T(8,128)}, f32[48,384]{1,0:T(8,128)S(1)}, u32[]{:S(2)}) copy-start(f32[48,384]{1,0:T(8,128)S(1)} %mul.344) | copy-start | bytes 221188
  19.4 322.3 %copy-start.49 = (pred[8]{0:T(512)(128)(4,1)}, pred[8]{0:T(512)(128)(4,1)S(1)}, u32[]{:S(2)}) copy-start(pred[8]{0:T(512)(128)(4,1)S(1)} %get-tuple-element.72) | copy-start | bytes 28
  19.7 348.5 %copy-start.47 = (pred[8]{0:T(512)(128)(4,1)}, pred[8]{0:T(512)(128)(4,1)S(1)}, u32[]{:S(2)}) copy-start(pred[8]{0:T(512)(128)(4,1)S(1)} %get-tuple-element.64) | copy-start | bytes 28
  19.7 351.2 %copy-start.45 = (pred[8]{0:T(512)(128)(4,1)}, pred[8]{0:T(512)(128)(4,1)S(1)}, u32[]{:S(2)}) copy-start(pred[8]{0:T(512)(128)(4,1)S(1)} %get-tuple-element.63) | copy-start | bytes 28
  241.4 73.7 %collective-permute-start.1 = (f32[1,8,2,432]{3,1,2,0:T(8,128)}, f32[1,8,2,432]{3,1,2,0:T(8,128)}, u32[]{:S(2)}, u32[]{:S(2)}) collective-permute-start(f32[1,8,2,432]{3,1,2,0:T(8,128)} %stack_reshape.22), channel_id=1, source_target_pairs={{16,0},{32,16},{48,32},{64,48},{80,64},{96,80},{112,96},{17,1},{33... | collective-permute-start | bytes 82952 | tf_op jit(solution)/shard_map/ppermute | solution.py:26
  247.8 51.8 %copy-start = (f32[7,48,8,48]{1,3,2,0:T(8,128)S(1)}, f32[7,48,8,48]{1,3,2,0:T(8,128)}, u32[]{:S(2)}) copy-start(f32[7,48,8,48]{1,3,2,0:T(8,128)} %fusion.48) | copy-start | bytes 1548292
  313.0 55.2 %copy-start.62 = (pred[8]{0:T(512)(128)(4,1)S(1)}, pred[8]{0:T(512)(128)(4,1)}, u32[]{:S(2)}) copy-start(pred[8]{0:T(512)(128)(4,1)} %get-tuple-element.225) | copy-start | bytes 28
  313.1 29.4 %collective-permute-start = (f32[1,8,2,432]{3,1,2,0:T(8,128)S(1)}, f32[1,8,2,432]{3,1,2,0:T(8,128)S(1)}, u32[]{:S(2)}, u32[]{:S(2)}) collective-permute-start(f32[1,8,2,432]{3,1,2,0:T(8,128)S(1)} %stack_reshape.21), channel_id=1, source_target_pairs={{0,16},{16,32},{32,48},{48,64},{64,80},{80,96},{96,112},{1,17},{17... | collective-permute-start | bytes 82952 | tf_op jit(solution)/shard_map/ppermute | solution.py:25
  339.3 31.6 %copy-start.59 = (pred[8]{0:T(512)(128)(4,1)S(1)}, pred[8]{0:T(512)(128)(4,1)}, u32[]{:S(2)}) copy-start(pred[8]{0:T(512)(128)(4,1)} %get-tuple-element.226) | copy-start | bytes 28
  342.4 33.2 %copy-start.4 = (f32[3,48,8,48]{3,2,1,0:T(8,128)S(1)}, f32[3,48,8,48]{3,2,1,0:T(8,128)}, u32[]{:S(2)}) copy-start(f32[3,48,8,48]{3,2,1,0:T(8,128)} %copy-done.3) | copy-start | bytes 663556
  477.2 31.0 %copy-start.80 = (pred[8]{0:T(512)(128)(4,1)S(1)}, pred[8]{0:T(512)(128)(4,1)}, u32[]{:S(2)}) copy-start(pred[8]{0:T(512)(128)(4,1)} %compare_and_fusion.3) | copy-start | bytes 28
  477.2 56.7 %copy-start.56 = (pred[8]{0:T(512)(128)(4,1)S(1)}, pred[8]{0:T(512)(128)(4,1)}, u32[]{:S(2)}) copy-start(pred[8]{0:T(512)(128)(4,1)} %get-tuple-element.68) | copy-start | bytes 28
  477.2 56.7 %copy-start.77 = (pred[8]{0:T(512)(128)(4,1)S(1)}, pred[8]{0:T(512)(128)(4,1)}, u32[]{:S(2)}) copy-start(pred[8]{0:T(512)(128)(4,1)} %compare_and_fusion.4) | copy-start | bytes 28
  479.2 59.0 %collective-permute-start.3 = (f32[1,8,2,336]{3,1,2,0:T(8,128)S(1)}, f32[1,8,2,336]{3,1,2,0:T(8,128)S(1)}, u32[]{:S(2)}, u32[]{:S(2)}) collective-permute-start(f32[1,8,2,336]{3,1,2,0:T(8,128)S(1)} %stack_reshape.24), channel_id=1, source_target_pairs={{16,0},{32,16},{48,32},{64,48},{80,64},{96,80},{112,96},{17,1},{33... | collective-permute-start | bytes 64520 | tf_op jit(solution)/shard_map/ppermute | solution.py:26
  534.0 63.3 %copy-start.54 = (pred[8]{0:T(512)(128)(4,1)S(1)}, pred[8]{0:T(512)(128)(4,1)}, u32[]{:S(2)}) copy-start(pred[8]{0:T(512)(128)(4,1)} %get-tuple-element.74) | copy-start | bytes 28
  534.0 63.3 %copy-start.69 = (pred[8]{0:T(512)(128)(4,1)S(1)}, pred[8]{0:T(512)(128)(4,1)}, u32[]{:S(2)}) copy-start(pred[8]{0:T(512)(128)(4,1)} %get-tuple-element.221) | copy-start | bytes 28
  534.1 63.8 %copy-start.52 = (pred[8]{0:T(512)(128)(4,1)S(1)}, pred[8]{0:T(512)(128)(4,1)}, u32[]{:S(2)}) copy-start(pred[8]{0:T(512)(128)(4,1)} %get-tuple-element.73) | copy-start | bytes 28
  534.1 63.8 %copy-start.66 = (pred[8]{0:T(512)(128)(4,1)S(1)}, pred[8]{0:T(512)(128)(4,1)}, u32[]{:S(2)}) copy-start(pred[8]{0:T(512)(128)(4,1)} %get-tuple-element.222) | copy-start | bytes 28
  536.2 63.6 %copy-start.50 = (pred[8]{0:T(512)(128)(4,1)S(1)}, pred[8]{0:T(512)(128)(4,1)}, u32[]{:S(2)}) copy-start(pred[8]{0:T(512)(128)(4,1)} %copy-done.49) | copy-start | bytes 28
  536.2 63.6 %copy-start.74 = (pred[8]{0:T(512)(128)(4,1)S(1)}, pred[8]{0:T(512)(128)(4,1)}, u32[]{:S(2)}) copy-start(pred[8]{0:T(512)(128)(4,1)} %compare_and_fusion.2) | copy-start | bytes 28
  536.3 32.3 %collective-permute-start.2 = (f32[1,8,2,336]{3,1,2,0:T(8,128)S(1)}, f32[1,8,2,336]{3,1,2,0:T(8,128)S(1)}, u32[]{:S(2)}, u32[]{:S(2)}) collective-permute-start(f32[1,8,2,336]{3,1,2,0:T(8,128)S(1)} %stack_reshape.23), channel_id=1, source_target_pairs={{0,16},{16,32},{32,48},{48,64},{64,80},{80,96},{96,112},{1,17},{17... | collective-permute-start | bytes 64520 | tf_op jit(solution)/shard_map/ppermute | solution.py:25
  563.4 37.1 %copy-start.48 = (pred[8]{0:T(512)(128)(4,1)S(1)}, pred[8]{0:T(512)(128)(4,1)}, u32[]{:S(2)}) copy-start(pred[8]{0:T(512)(128)(4,1)} %copy-done.47) | copy-start | bytes 28
  563.5 37.1 %copy-start.63 = (pred[8]{0:T(512)(128)(4,1)S(1)}, pred[8]{0:T(512)(128)(4,1)}, u32[]{:S(2)}) copy-start(pred[8]{0:T(512)(128)(4,1)} %get-tuple-element.225) | copy-start | bytes 28
  565.2 36.0 %copy-start.46 = (pred[8]{0:T(512)(128)(4,1)S(1)}, pred[8]{0:T(512)(128)(4,1)}, u32[]{:S(2)}) copy-start(pred[8]{0:T(512)(128)(4,1)} %copy-done.45) | copy-start | bytes 28
  565.2 36.0 %copy-start.60 = (pred[8]{0:T(512)(128)(4,1)S(1)}, pred[8]{0:T(512)(128)(4,1)}, u32[]{:S(2)}) copy-start(pred[8]{0:T(512)(128)(4,1)} %get-tuple-element.226) | copy-start | bytes 28
  625.8 50.8 %copy-start.78 = (pred[8]{0:T(512)(128)(4,1)S(1)}, pred[8]{0:T(512)(128)(4,1)}, u32[]{:S(2)}) copy-start(pred[8]{0:T(512)(128)(4,1)} %compare_and_fusion.4) | copy-start | bytes 28
  627.8 53.1 %collective-permute-start.5 = (f32[1,8,2,336]{3,1,2,0:T(8,128)S(1)}, f32[1,8,2,336]{3,1,2,0:T(8,128)S(1)}, u32[]{:S(2)}, u32[]{:S(2)}) collective-permute-start(f32[1,8,2,336]{3,1,2,0:T(8,128)S(1)} %stack_reshape.26), channel_id=1, source_target_pairs={{16,0},{32,16},{48,32},{64,48},{80,64},{96,80},{112,96},{17,1},{33... | collective-permute-start | bytes 64520 | tf_op jit(solution)/shard_map/ppermute | solution.py:26
  676.7 53.8 %copy-start.70 = (pred[8]{0:T(512)(128)(4,1)S(1)}, pred[8]{0:T(512)(128)(4,1)}, u32[]{:S(2)}) copy-start(pred[8]{0:T(512)(128)(4,1)} %get-tuple-element.221) | copy-start | bytes 28
  676.9 54.3 %copy-start.67 = (pred[8]{0:T(512)(128)(4,1)S(1)}, pred[8]{0:T(512)(128)(4,1)}, u32[]{:S(2)}) copy-start(pred[8]{0:T(512)(128)(4,1)} %get-tuple-element.222) | copy-start | bytes 28
  678.9 54.1 %copy-start.75 = (pred[8]{0:T(512)(128)(4,1)S(1)}, pred[8]{0:T(512)(128)(4,1)}, u32[]{:S(2)}) copy-start(pred[8]{0:T(512)(128)(4,1)} %compare_and_fusion.2) | copy-start | bytes 28
  679.0 27.6 %collective-permute-start.4 = (f32[1,8,2,336]{3,1,2,0:T(8,128)S(1)}, f32[1,8,2,336]{3,1,2,0:T(8,128)S(1)}, u32[]{:S(2)}, u32[]{:S(2)}) collective-permute-start(f32[1,8,2,336]{3,1,2,0:T(8,128)S(1)} %stack_reshape.25), channel_id=1, source_target_pairs={{0,16},{16,32},{32,48},{48,64},{64,80},{80,96},{96,112},{1,17},{17... | collective-permute-start | bytes 64520 | tf_op jit(solution)/shard_map/ppermute | solution.py:25
  (60 other events, 567.6 us)
Sparse Core Ops, SparseCore 0:
  11.8 220.8 all-gather.7
where the time goes:
time: 778 us; the launch traced here: 768 us
  blocking collectives  285 us (37%)
  waiting for transfers between devices  210 us (27%)
  local copies, waits for them, and re-layouts  187 us (24%)
  other arithmetic  58.8 us (8%)
  between operations  16.6 us (2%)
  starting transfers between devices  11.7 us (2%)
    all_gather x12, blocking collectives, move_along(): return lax.all_gather(members, 'gy', axis=0, tiled=True)  285 us
    all_gather x1, waiting for transfers between devices, relocate(): portion = lax.all_gather(columns_flat, 'gy', axis=1, tiled=True)  210 us
    concatenate x36, local copies, waits for them, and re-layouts, rolled(): return jnp.roll(field, (-north, -east), axis=(-2, -1))  36.7 us
    gather x24, local copies, waits for them, and re-layouts, pick(): chosen = jnp.take(rim_pool, position, axis=0)  30.4 us
    unnamed x212, local copies, waits for them, and re-layouts  22.2 us
    slice x46, local copies, waits for them, and re-layouts, rolled(): return jnp.roll(field, (-north, -east), axis=(-2, -1))  20.7 us
  transfers between devices with their start and end apart: 7, of which 1 were waited for; matrix products, arithmetic and copies ran while one was open for 7% of the time, Pallas kernels for 0%

commit v1 on v0

--- a/solution.py
+++ b/solution.py
@@ -13,6 +13,13 @@
 coriolis_amp = 0.5
 surface_coef = 0.5
 gravity_coef = 0.5
+
+
+def exchange_gather(value, name, dim):
+    size = lax.axis_size(name)
+    shards = jnp.stack([value for _ in range(size)])
+    shards = lax.all_to_all(shards, name, split_axis=0, concat_axis=0)
+    return jnp.concatenate(shards, axis=dim)
 
 
 def with_halo(value, sides, width):
@@ -219,7 +226,7 @@
     in_use = slot_ids >= 0
     column = jnp.where(in_use, slot_ids % blocks_east, -1)
     initial = jnp.zeros((channels * tile_length, slot_count, tile_length), jnp.float32)
-    portion = lax.all_gather(columns_flat, "gy", axis=1, tiled=True)
+    portion = exchange_gather(columns_flat, "gy", 1)
     portion_blocks = portion.shape[1] // tile_length
     usable = in_use & (column >= 0) & (column < portion_blocks)
     taken = jnp.take(

time: 778 us -> 1090 us (1.40)
  waiting for transfers between devices: 210 us -> 483 us
  local copies, waits for them, and re-layouts: 187 us -> 228 us
  between operations: 16.6 us -> 3.23 us
    all_to_all x0 -> x1, waiting for transfers between devices: none -> 483 us  [exchange_gather(): shards = lax.all_to_all(shards, name, split_axis=0, concat_axis=0)]
    all_gather x1 -> x0, waiting for transfers between devices: 210 us -> none  [relocate(): portion = lax.all_gather(columns_flat, 'gy', axis=1, tiled=True)]
    reshape x1, local copies, waits for them, and re-layouts: 1.96 us -> 35.1 us  [exchange_gather(): return jnp.concatenate(shards, axis=dim)]
    another operation x0 -> x1, local copies, waits for them, and re-layouts: none -> 11 us  [exchange_gather(): shards = jnp.stack([value for _ in range(size)])]
    unnamed x212 -> x210, local copies, waits for them, and re-layouts: 22.2 us -> 20.8 us
  transfers between devices with their start and end apart: 7 -> 7, of which waited for: 1 -> 1; matrix products, arithmetic and copies ran while one was open for 7% -> 5% of each run, Pallas kernels for 0% -> 0%
where the time goes in v1:
time: 1090 us; the launch traced here: 1080 us
  waiting for transfers between devices  483 us (44%)
  blocking collectives  284 us (26%)
  local copies, waits for them, and re-layouts  228 us (21%)
  other arithmetic  57.2 us (5%)
  starting transfers between devices  19.7 us (2%)
    all_to_all x1, waiting for transfers between devices, exchange_gather(): shards = lax.all_to_all(shards, name, split_axis=0, concat_axis=0)  483 us
    all_gather x12, blocking collectives, move_along(): return lax.all_gather(members, 'gy', axis=0, tiled=True)  284 us
    concatenate x36, local copies, waits for them, and re-layouts, rolled(): return jnp.roll(field, (-north, -east), axis=(-2, -1))  36.7 us
    reshape x1, local copies, waits for them, and re-layouts, exchange_gather(): return jnp.concatenate(shards, axis=dim)  35.1 us
    gather x24, local copies, waits for them, and re-layouts, pick(): chosen = jnp.take(rim_pool, position, axis=0)  30.4 us
  transfers between devices with their start and end apart: 7, of which 1 were waited for; matrix products, arithmetic and copies ran while one was open for 5% of the time, Pallas kernels for 0%

profile of v1, /device:TPU:6, one launch (start us, length us, event | category | flops | bytes accessed | tf_op | source)
XLA Modules:
  0.0 1075.6 jit_solution(8670310719588218627)
XLA Ops:
  3.1 11.0 %stack.44 = f32[16,672,768]{2,1,0:T(8,128)} broadcast(f32[672,768]{1,0:T(8,128)S(1)} %bitcast.225), dimensions={1,2} | broadcast | bytes 35094528 | tf_op jit(solution)/shard_map/stack | solution.py:20
  14.1 8.2 all-to-all-start
  33.1 483.3 %all-to-all-done = f32[16,672,768]{2,1,0:T(8,128)} async-done(((f32[16,672,768]{2,1,0:T(8,128)}), f32[16,672,768]{2,1,0:T(8,128)}, u32[]{:S(2)}, u32[]{:S(2)}) %all-to-all-start) | async-done | bytes 33030176 | tf_op jit(solution)/shard_map/all_to_all | solution.py:21
  516.4 35.1 %copy.539 = f32[672,16,768]{0,2,1:T(8,128)} copy(f32[672,16,768]{2,0,1:T(8,128)} %bitcast.6) | data formatting | bytes 66060288 | tf_op jit(solution)/shard_map/reshape | solution.py:22
  562.2 2.3 fusion.73
  566.6 23.6 %all_gather.38 = f32[128,2,432]{2,1,0:T(2,128)} all-gather(f32[8,2,432]{2,1,0:T(2,128)S(1)} %copy.559), channel_id=1, replica_groups=mesh['gx'=8,'gy'=16] {'gy'}, dimensions={0}, use_global_device_ids=true | all-gather | bytes 470016 | tf_op jit(solution)/shard_map/all_gather | solution.py:378
  592.2 25.4 %all_gather.37 = f32[128,2,432]{2,1,0:T(2,128)} all-gather(f32[8,2,432]{2,1,0:T(2,128)S(1)} %copy.555), channel_id=1, replica_groups=mesh['gx'=8,'gy'=16] {'gy'}, dimensions={0}, use_global_device_ids=true | all-gather | bytes 470016 | tf_op jit(solution)/shard_map/all_gather | solution.py:378
  633.9 21.5 %all-gather.1 = f32[1,128,2,432]{3,2,0,1:T(2,128)S(1)} all-gather(f32[1,8,2,432]{3,2,0,1:T(2,128)S(1)} %copy.563), channel_id=3, replica_groups=mesh['gx'=8,'gy'=16] {'gy'}, dimensions={1}, use_global_device_ids=true | all-gather | bytes 470016 | tf_op jit(solution)/shard_map/all_gather | solution.py:378
  658.7 25.9 %all-gather = f32[1,128,2,432]{3,2,0,1:T(2,128)} all-gather(f32[1,8,2,432]{3,2,0,1:T(2,128)S(1)} %copy.547), channel_id=2, replica_groups=mesh['gx'=8,'gy'=16] {'gy'}, dimensions={1}, use_global_device_ids=true | all-gather | bytes 470016 | tf_op jit(solution)/shard_map/all_gather | solution.py:378
  693.9 3.4 pad_maximum_fusion
  718.7 2.2 add.250
  721.7 2.1 concatenate.309
  726.3 3.0 fusion.1
  733.1 2.1 concatenate.305
  736.6 2.4 fusion.4
  741.0 2.5 fusion.18
  743.5 2.1 div.43
  752.4 2.2 concatenate.283
  760.4 2.2 concatenate.299
  764.7 2.1 concatenate.295
  768.8 2.1 add.244
  773.5 5.6 fusion.11
  790.4 2.5 subtract_reduce_fusion
  799.5 23.3 %all_gather.42 = f32[128,2,336]{2,1,0:T(2,128)} all-gather(f32[8,2,336]{2,1,0:T(2,128)S(1)} %reshape.802), channel_id=1, replica_groups=mesh['gx'=8,'gy'=16] {'gy'}, dimensions={0}, use_global_device_ids=true | all-gather | bytes 365568 | tf_op jit(solution)/shard_map/all_gather | solution.py:390
  824.7 25.6 %all_gather.41 = f32[128,2,336]{2,1,0:T(2,128)} all-gather(f32[8,2,336]{2,1,0:T(2,128)S(1)} %reshape.800), channel_id=1, replica_groups=mesh['gx'=8,'gy'=16] {'gy'}, dimensions={0}, use_global_device_ids=true | all-gather | bytes 365568 | tf_op jit(solution)/shard_map/all_gather | solution.py:390
  856.4 23.3 %all-gather.3 = f32[1,128,2,336]{3,2,0,1:T(2,128)} all-gather(f32[1,8,2,336]{3,2,0,1:T(2,128)S(1)} %copy.594), channel_id=5, replica_groups=mesh['gx'=8,'gy'=16] {'gy'}, dimensions={1}, use_global_device_ids=true | all-gather | bytes 365568 | tf_op jit(solution)/shard_map/all_gather | solution.py:390
  884.9 25.3 %all-gather.2 = f32[1,128,2,336]{3,2,0,1:T(2,128)} all-gather(f32[1,8,2,336]{3,2,0,1:T(2,128)S(1)} %copy.578), channel_id=4, replica_groups=mesh['gx'=8,'gy'=16] {'gy'}, dimensions={1}, use_global_device_ids=true | all-gather | bytes 365568 | tf_op jit(solution)/shard_map/all_gather | solution.py:390
  947.9 21.4 %all_gather.46 = f32[128,2,336]{2,1,0:T(2,128)S(1)} all-gather(f32[8,2,336]{2,1,0:T(2,128)S(1)} %reshape.817), channel_id=1, replica_groups=mesh['gx'=8,'gy'=16] {'gy'}, dimensions={0}, use_global_device_ids=true | all-gather | bytes 365568 | tf_op jit(solution)/shard_map/all_gather | solution.py:390
  970.3 23.4 %all_gather.45 = f32[128,2,336]{2,1,0:T(2,128)S(1)} all-gather(f32[8,2,336]{2,1,0:T(2,128)S(1)} %reshape.815), channel_id=1, replica_groups=mesh['gx'=8,'gy'=16] {'gy'}, dimensions={0}, use_global_device_ids=true | all-gather | bytes 365568 | tf_op jit(solution)/shard_map/all_gather | solution.py:390
  998.9 21.8 %all-gather.5 = f32[1,128,2,336]{3,2,0,1:T(2,128)S(1)} all-gather(f32[1,8,2,336]{3,2,0,1:T(2,128)S(1)} %copy.631), channel_id=7, replica_groups=mesh['gx'=8,'gy'=16] {'gy'}, dimensions={1}, use_global_device_ids=true | all-gather | bytes 365568 | tf_op jit(solution)/shard_map/all_gather | solution.py:390
  1022.9 23.4 %all-gather.4 = f32[1,128,2,336]{3,2,0,1:T(2,128)S(1)} all-gather(f32[1,8,2,336]{3,2,0,1:T(2,128)S(1)} %copy.615), channel_id=6, replica_groups=mesh['gx'=8,'gy'=16] {'gy'}, dimensions={1}, use_global_device_ids=true | all-gather | bytes 365568 | tf_op jit(solution)/shard_map/all_gather | solution.py:390
  1067.6 2.6 fusion.21
  (534 shorter events, 209.3 us)
Async XLA Ops:
  14.1 502.3 %all-to-all-start = ((f32[16,672,768]{2,1,0:T(8,128)}), f32[16,672,768]{2,1,0:T(8,128)}, u32[]{:S(2)}, u32[]{:S(2)}) async-start(f32[16,672,768]{2,1,0:T(8,128)} %stack.44), calls=%async_computation | async-start | bytes 66060288 | tf_op jit(solution)/shard_map/all_to_all | solution.py:21
  22.9 528.7 %copy-start.30 = (f32[48,384]{1,0:T(8,128)}, f32[48,384]{1,0:T(8,128)S(1)}, u32[]{:S(2)}) copy-start(f32[48,384]{1,0:T(8,128)S(1)} %mul.344) | copy-start | bytes 221188
  29.5 628.5 %copy-start.48 = (pred[8]{0:T(512)(128)(4,1)}, pred[8]{0:T(512)(128)(4,1)S(1)}, u32[]{:S(2)}) copy-start(pred[8]{0:T(512)(128)(4,1)S(1)} %get-tuple-element.72) | copy-start | bytes 28
  29.7 656.6 %copy-start.46 = (pred[8]{0:T(512)(128)(4,1)}, pred[8]{0:T(512)(128)(4,1)S(1)}, u32[]{:S(2)}) copy-start(pred[8]{0:T(512)(128)(4,1)S(1)} %get-tuple-element.64) | copy-start | bytes 28
  29.7 659.3 %copy-start.44 = (pred[8]{0:T(512)(128)(4,1)}, pred[8]{0:T(512)(128)(4,1)S(1)}, u32[]{:S(2)}) copy-start(pred[8]{0:T(512)(128)(4,1)S(1)} %get-tuple-element.63) | copy-start | bytes 28
  560.2 72.9 %collective-permute-start.1 = (f32[1,8,2,432]{3,1,2,0:T(8,128)}, f32[1,8,2,432]{3,1,2,0:T(8,128)}, u32[]{:S(2)}, u32[]{:S(2)}) collective-permute-start(f32[1,8,2,432]{3,1,2,0:T(8,128)} %stack_reshape.16), channel_id=1, source_target_pairs={{16,0},{32,16},{48,32},{64,48},{80,64},{96,80},{112,96},{17,1},{33... | collective-permute-start | bytes 82952 | tf_op jit(solution)/shard_map/ppermute | solution.py:33
  566.6 51.1 %copy-start = (f32[7,48,8,48]{1,3,2,0:T(8,128)S(1)}, f32[7,48,8,48]{1,3,2,0:T(8,128)}, u32[]{:S(2)}) copy-start(f32[7,48,8,48]{1,3,2,0:T(8,128)} %fusion.48) | copy-start | bytes 1548292
  590.1 31.6 %copy-start.56 = (pred[8]{0:T(512)(128)(4,1)S(1)}, pred[8]{0:T(512)(128)(4,1)}, u32[]{:S(2)}) copy-start(pred[8]{0:T(512)(128)(4,1)} %get-tuple-element.69) | copy-start | bytes 28
  631.1 55.3 %copy-start.61 = (pred[8]{0:T(512)(128)(4,1)S(1)}, pred[8]{0:T(512)(128)(4,1)}, u32[]{:S(2)}) copy-start(pred[8]{0:T(512)(128)(4,1)} %get-tuple-element.225) | copy-start | bytes 28
  631.2 27.5 %collective-permute-start = (f32[1,8,2,432]{3,1,2,0:T(8,128)S(1)}, f32[1,8,2,432]{3,1,2,0:T(8,128)S(1)}, u32[]{:S(2)}, u32[]{:S(2)}) collective-permute-start(f32[1,8,2,432]{3,1,2,0:T(8,128)S(1)} %stack_reshape.15), channel_id=1, source_target_pairs={{0,16},{16,32},{32,48},{48,64},{64,80},{80,96},{96,112},{1,17},{17... | collective-permute-start | bytes 82952 | tf_op jit(solution)/shard_map/ppermute | solution.py:32
  655.5 33.6 %copy-start.58 = (pred[8]{0:T(512)(128)(4,1)S(1)}, pred[8]{0:T(512)(128)(4,1)}, u32[]{:S(2)}) copy-start(pred[8]{0:T(512)(128)(4,1)} %get-tuple-element.226) | copy-start | bytes 28
  658.6 35.2 %copy-start.4 = (f32[3,48,8,48]{3,2,1,0:T(8,128)S(1)}, f32[3,48,8,48]{3,2,1,0:T(8,128)}, u32[]{:S(2)}) copy-start(f32[3,48,8,48]{3,2,1,0:T(8,128)} %copy-done.3) | copy-start | bytes 663556
  795.3 56.7 %copy-start.55 = (pred[8]{0:T(512)(128)(4,1)S(1)}, pred[8]{0:T(512)(128)(4,1)}, u32[]{:S(2)}) copy-start(pred[8]{0:T(512)(128)(4,1)} %get-tuple-element.68) | copy-start | bytes 28
  795.3 56.7 %copy-start.76 = (pred[8]{0:T(512)(128)(4,1)S(1)}, pred[8]{0:T(512)(128)(4,1)}, u32[]{:S(2)}) copy-start(pred[8]{0:T(512)(128)(4,1)} %compare_and_fusion.4) | copy-start | bytes 28
  797.4 59.0 %collective-permute-start.3 = (f32[1,8,2,336]{3,1,2,0:T(8,128)S(1)}, f32[1,8,2,336]{3,1,2,0:T(8,128)S(1)}, u32[]{:S(2)}, u32[]{:S(2)}) collective-permute-start(f32[1,8,2,336]{3,1,2,0:T(8,128)S(1)} %stack_reshape.18), channel_id=1, source_target_pairs={{16,0},{32,16},{48,32},{64,48},{80,64},{96,80},{112,96},{17,1},{33... | collective-permute-start | bytes 64520 | tf_op jit(solution)/shard_map/ppermute | solution.py:33
  852.1 63.2 %copy-start.53 = (pred[8]{0:T(512)(128)(4,1)S(1)}, pred[8]{0:T(512)(128)(4,1)}, u32[]{:S(2)}) copy-start(pred[8]{0:T(512)(128)(4,1)} %get-tuple-element.74) | copy-start | bytes 28
  852.1 63.2 %copy-start.68 = (pred[8]{0:T(512)(128)(4,1)S(1)}, pred[8]{0:T(512)(128)(4,1)}, u32[]{:S(2)}) copy-start(pred[8]{0:T(512)(128)(4,1)} %get-tuple-element.221) | copy-start | bytes 28
  852.3 63.8 %copy-start.51 = (pred[8]{0:T(512)(128)(4,1)S(1)}, pred[8]{0:T(512)(128)(4,1)}, u32[]{:S(2)}) copy-start(pred[8]{0:T(512)(128)(4,1)} %get-tuple-element.73) | copy-start | bytes 28
  852.3 63.7 %copy-start.65 = (pred[8]{0:T(512)(128)(4,1)S(1)}, pred[8]{0:T(512)(128)(4,1)}, u32[]{:S(2)}) copy-start(pred[8]{0:T(512)(128)(4,1)} %get-tuple-element.222) | copy-start | bytes 28
  854.3 63.5 %copy-start.49 = (pred[8]{0:T(512)(128)(4,1)S(1)}, pred[8]{0:T(512)(128)(4,1)}, u32[]{:S(2)}) copy-start(pred[8]{0:T(512)(128)(4,1)} %copy-done.48) | copy-start | bytes 28
  854.3 63.5 %copy-start.73 = (pred[8]{0:T(512)(128)(4,1)S(1)}, pred[8]{0:T(512)(128)(4,1)}, u32[]{:S(2)}) copy-start(pred[8]{0:T(512)(128)(4,1)} %compare_and_fusion.2) | copy-start | bytes 28
  854.4 30.4 %collective-permute-start.2 = (f32[1,8,2,336]{3,1,2,0:T(8,128)S(1)}, f32[1,8,2,336]{3,1,2,0:T(8,128)S(1)}, u32[]{:S(2)}, u32[]{:S(2)}) collective-permute-start(f32[1,8,2,336]{3,1,2,0:T(8,128)S(1)} %stack_reshape.17), channel_id=1, source_target_pairs={{0,16},{16,32},{32,48},{48,64},{64,80},{80,96},{96,112},{1,17},{17... | collective-permute-start | bytes 64520 | tf_op jit(solution)/shard_map/ppermute | solution.py:32
  879.7 38.9 %copy-start.47 = (pred[8]{0:T(512)(128)(4,1)S(1)}, pred[8]{0:T(512)(128)(4,1)}, u32[]{:S(2)}) copy-start(pred[8]{0:T(512)(128)(4,1)} %copy-done.46) | copy-start | bytes 28
  879.7 38.9 %copy-start.62 = (pred[8]{0:T(512)(128)(4,1)S(1)}, pred[8]{0:T(512)(128)(4,1)}, u32[]{:S(2)}) copy-start(pred[8]{0:T(512)(128)(4,1)} %get-tuple-element.225) | copy-start | bytes 28
  881.5 37.8 %copy-start.45 = (pred[8]{0:T(512)(128)(4,1)S(1)}, pred[8]{0:T(512)(128)(4,1)}, u32[]{:S(2)}) copy-start(pred[8]{0:T(512)(128)(4,1)} %copy-done.44) | copy-start | bytes 28
  881.5 37.8 %copy-start.59 = (pred[8]{0:T(512)(128)(4,1)S(1)}, pred[8]{0:T(512)(128)(4,1)}, u32[]{:S(2)}) copy-start(pred[8]{0:T(512)(128)(4,1)} %get-tuple-element.226) | copy-start | bytes 28
  943.8 50.7 %copy-start.77 = (pred[8]{0:T(512)(128)(4,1)S(1)}, pred[8]{0:T(512)(128)(4,1)}, u32[]{:S(2)}) copy-start(pred[8]{0:T(512)(128)(4,1)} %compare_and_fusion.4) | copy-start | bytes 28
  945.9 52.9 %collective-permute-start.5 = (f32[1,8,2,336]{3,1,2,0:T(8,128)S(1)}, f32[1,8,2,336]{3,1,2,0:T(8,128)S(1)}, u32[]{:S(2)}, u32[]{:S(2)}) collective-permute-start(f32[1,8,2,336]{3,1,2,0:T(8,128)S(1)} %stack_reshape.20), channel_id=1, source_target_pairs={{16,0},{32,16},{48,32},{64,48},{80,64},{96,80},{112,96},{17,1},{33... | collective-permute-start | bytes 64520 | tf_op jit(solution)/shard_map/ppermute | solution.py:33
  994.6 53.8 %copy-start.69 = (pred[8]{0:T(512)(128)(4,1)S(1)}, pred[8]{0:T(512)(128)(4,1)}, u32[]{:S(2)}) copy-start(pred[8]{0:T(512)(128)(4,1)} %get-tuple-element.221) | copy-start | bytes 28
  994.7 54.3 %copy-start.66 = (pred[8]{0:T(512)(128)(4,1)S(1)}, pred[8]{0:T(512)(128)(4,1)}, u32[]{:S(2)}) copy-start(pred[8]{0:T(512)(128)(4,1)} %get-tuple-element.222) | copy-start | bytes 28
  996.8 54.1 %copy-start.74 = (pred[8]{0:T(512)(128)(4,1)S(1)}, pred[8]{0:T(512)(128)(4,1)}, u32[]{:S(2)}) copy-start(pred[8]{0:T(512)(128)(4,1)} %compare_and_fusion.2) | copy-start | bytes 28
  996.9 26.0 %collective-permute-start.4 = (f32[1,8,2,336]{3,1,2,0:T(8,128)S(1)}, f32[1,8,2,336]{3,1,2,0:T(8,128)S(1)}, u32[]{:S(2)}, u32[]{:S(2)}) collective-permute-start(f32[1,8,2,336]{3,1,2,0:T(8,128)S(1)} %stack_reshape.19), channel_id=1, source_target_pairs={{0,16},{16,32},{32,48},{48,64},{64,80},{80,96},{96,112},{1,17},{17... | collective-permute-start | bytes 64520 | tf_op jit(solution)/shard_map/ppermute | solution.py:32
  (59 other events, 558.0 us)
